TPU v7x, 256 devices: a whole 4x4x8 slice. The times are simulated.
256 devices in a mesh: wide: 64 (over z, y, core), narrow: 4 (over x).
Axes of the slice: x: 4, y: 4, z: 8, core: 2. Of those that a mesh axis runs over, the one named last changes fastest.
Arguments:
- hidden_in: bfloat16 [1024, 4096], P('narrow', 'wide'), may hold values from -0.59765625 to 0.59765625
- cached_len: int32 [4], replicated, may hold values from 1 to 4096, 8192 in all
- k_cache: bfloat16 [4, 32768, 128], P('narrow', 'wide'), may hold values from -256 to 256
- v_cache: bfloat16 [4, 32768, 128], P('narrow', 'wide'), may hold values from -24 to 24
- attn_gain: bfloat16 [4096], replicated, may hold values from 0.099609375 to 1.8984375
- ffn_gain: bfloat16 [4096], replicated, may hold values from 0.099609375 to 1.8984375
- wqkv: bfloat16 [6144, 4096], P('wide', 'narrow'), may hold values from -0.09375 to 0.09375
- wo: bfloat16 [4096, 4096], P('wide', 'narrow'), may hold values from -0.09375 to 0.09375
- wgate: bfloat16 [14336, 4096], P('wide', 'narrow'), may hold values from -0.09375 to 0.09375
- wup: bfloat16 [14336, 4096], P('wide', 'narrow'), may hold values from -0.09375 to 0.09375
- wdown: bfloat16 [14336, 4096], P('wide', 'narrow'), may hold values from -0.125 to 0.125
Outputs:
- hidden_out: bfloat16 [1024, 4096], P('narrow', 'wide')
- new_k_cache: bfloat16 [4, 32768, 128], P('narrow', 'wide')
- new_v_cache: bfloat16 [4, 32768, 128], P('narrow', 'wide')
All inputs are finite; a program needn't handle non-finite values.
Results may differ from a plain program's by a relative error of at most 0.018.
The roundings to bfloat16 on the way count: a program that leaves them out, or rounds other values in their place, can miss the bound.
Values may be sent and summed in bfloat16 or wider, within the bound.
A program may use at most 64 MiB of HBM per device.

v0:
```python
import jax
import jax.numpy as jnp
from jax import lax
from jax.sharding import PartitionSpec as P

QH = 32
KVH = 8
HD = 128
WINDOW = 4096
NEG_FILL = -1e30


def partner(block, axis, stride):
    count = lax.axis_size(axis)
    route = []
    for low in range(count):
        high = low | 1 << stride
        if high != low and high < count:
            route += [(low, high), (high, low)]
    return lax.ppermute(block, axis, route)


def rms_scale(values, weights):
    widened = values.astype(jnp.float32)
    mean_square = jnp.mean(widened * widened, axis=-1, keepdims=True)
    return (widened * lax.rsqrt(mean_square + 1e-05) * weights.astype(jnp.float32)).astype(
        jnp.bfloat16
    )


def times_rows(left, right):
    return lax.dot_general(
        left, right, (((1,), (1,)), ((), ())), preferred_element_type=jnp.float32
    )


def rotate(heads, positions):
    half_width = heads.shape[-1] // 2
    exponent = jnp.arange(half_width, dtype=jnp.float32) * (2.0 / heads.shape[-1])
    frequency = jnp.power(10000.0, -exponent)
    angles = positions.astype(jnp.float32)[:, None] * frequency[None, :]
    cosine = jnp.cos(angles)[:, None, :]
    sine = jnp.sin(angles)[:, None, :]
    widened = heads.astype(jnp.float32)
    first_half = widened[..., :half_width]
    second_half = widened[..., half_width:]
    return jnp.concatenate(
        [first_half * cosine - second_half * sine, second_half * cosine + first_half * sine],
        axis=-1,
    ).astype(jnp.bfloat16)


def gather_cols(block):
    return lax.all_gather(block, "wide", axis=1, tiled=True)


def collect_heads(qkv_piece, sections):
    position = lax.axis_index("wide")
    for bit_index in range(sections):
        other_piece = partner(qkv_piece, "wide", bit_index)
        upper_half = position // 2**bit_index % 2 == 1
        qkv_piece = jnp.where(
            upper_half,
            jnp.concatenate([other_piece, qkv_piece], axis=1),
            jnp.concatenate([qkv_piece, other_piece], axis=1),
        )
    return qkv_piece


def combine(earlier, later):
    highest = jnp.maximum(earlier[0], later[0])
    left_scale = jnp.exp(earlier[0] - highest)
    right_scale = jnp.exp(later[0] - highest)
    return (
        highest,
        earlier[1] * left_scale + later[1] * right_scale,
        earlier[2] * left_scale[..., None] + later[2] * right_scale[..., None],
    )


def empty_state(row_count, group_size):
    return (
        jnp.full((row_count, group_size), NEG_FILL, jnp.float32),
        jnp.zeros((row_count, group_size), jnp.float32),
        jnp.zeros((row_count, group_size, HD), jnp.float32),
    )


def attend(queries, query_pos, keys, values, key_pos, key_live, soft_state):
    row_count, group_size, head_width = queries.shape
    flat_queries = queries.reshape(row_count * group_size, head_width)
    key_count = keys.shape[0]
    block_size = min(512, key_count)
    block_count = key_count // block_size
    lowest = jnp.min(query_pos)
    highest = jnp.max(query_pos)

    def key_step(carry, blocks):
        key_block, value_block, pos_block, live_block = blocks

        def score_block(running):
            peak_old, totals, accum = running
            scores = jnp.einsum(
                "qd,kd->qk", flat_queries, key_block, preferred_element_type=jnp.float32
            )
            scores = scores.reshape(row_count, group_size, block_size) * HD ** (-0.5)
            allowed = (
                live_block[None, :]
                & (pos_block[None, :] <= query_pos[:, None])
                & (pos_block[None, :] > query_pos[:, None] - WINDOW)
            )
            allowed = allowed[:, None, :]
            scores = jnp.where(allowed, scores, NEG_FILL)
            peak_new = jnp.maximum(peak_old, jnp.max(scores, axis=-1))
            factor = jnp.exp(peak_old - peak_new)
            exp_terms = jnp.where(allowed, jnp.exp(scores - peak_new[..., None]), 0.0)
            totals = totals * factor + jnp.sum(exp_terms, axis=-1)
            weights = exp_terms.astype(jnp.bfloat16).reshape(row_count * group_size, block_size)
            mixed = jnp.dot(weights, value_block, preferred_element_type=jnp.float32).reshape(
                row_count, group_size, head_width
            )
            return (peak_new, totals, accum * factor[..., None] + mixed)

        useful = jnp.any(live_block & (pos_block <= highest) & (pos_block > lowest - WINDOW))
        return (lax.cond(useful, score_block, lambda unchanged: unchanged, carry), None)

    blocks = (
        keys.reshape(block_count, block_size, head_width),
        values.reshape(block_count, block_size, head_width),
        key_pos.reshape(block_count, block_size),
        key_live.reshape(block_count, block_size),
    )
    soft_state, _ = lax.scan(key_step, soft_state, blocks)
    return soft_state


def per_device(
    hidden_in, cached_len, k_cache, v_cache, attn_gain, ffn_gain, wqkv, wo, wgate, wup, wdown
):
    qkv_full, out_full, gate_full, up_full, down_full = (
        lax.all_gather(wqkv, "narrow", axis=1, tiled=True),
        lax.all_gather(wo, "narrow", axis=1, tiled=True),
        lax.all_gather(wgate, "narrow", axis=1, tiled=True),
        lax.all_gather(wup, "narrow", axis=1, tiled=True),
        lax.all_gather(wdown, "narrow", axis=1, tiled=True),
    )
    wide_count = lax.axis_size("wide")
    part_count = wide_count // KVH
    sections = part_count.bit_length() - 1
    position = lax.axis_index("wide")
    part_index = position % part_count
    length = cached_len[lax.axis_index("narrow")]
    span_len = hidden_in.shape[0]
    group_size = QH // KVH
    steps_t = jnp.arange(span_len, dtype=jnp.int32)
    query_pos = length + steps_t
    normed_attn = rms_scale(gather_cols(hidden_in), attn_gain)
    qkv_piece = times_rows(normed_attn, qkv_full).astype(jnp.bfloat16)
    grouped = collect_heads(qkv_piece, sections)
    queries = rotate(grouped[:, : group_size * HD].reshape(span_len, group_size, HD), query_pos)
    new_keys = rotate(
        grouped[:, group_size * HD : (group_size + 1) * HD].reshape(span_len, 1, HD), query_pos
    ).reshape(span_len, HD)
    new_vals = grouped[:, (group_size + 1) * HD :]
    cache_keys = k_cache[0]
    cache_vals = v_cache[0]
    block_slots = cache_keys.shape[0]
    slot_pos = part_index * block_slots + jnp.arange(block_slots, dtype=jnp.int32)
    share_rows = span_len // part_count
    start_row = part_index * share_rows
    soft_state = empty_state(span_len, group_size)
    soft_state = attend(
        queries, query_pos, cache_keys, cache_vals, slot_pos, slot_pos < length, soft_state
    )
    soft_state = attend(
        queries,
        query_pos,
        lax.dynamic_slice_in_dim(new_keys, start_row, share_rows, 0),
        lax.dynamic_slice_in_dim(new_vals, start_row, share_rows, 0),
        lax.dynamic_slice_in_dim(query_pos, start_row, share_rows, 0),
        jnp.ones((share_rows,), jnp.bool_),
        soft_state,
    )
    for bit_index in range(sections):
        soft_state = combine(soft_state, partner(soft_state, "wide", bit_index))
    attended = (
        (soft_state[2] / soft_state[1][..., None])
        .astype(jnp.bfloat16)
        .reshape(span_len, group_size * HD)
    )
    width_share = group_size * HD // part_count
    own_cols = lax.dynamic_slice_in_dim(attended, part_index * width_share, width_share, 1)
    mixed_heads = gather_cols(own_cols)
    projected = times_rows(mixed_heads, out_full)
    after_attn = (hidden_in.astype(jnp.float32) + projected).astype(jnp.bfloat16)
    whole_after = gather_cols(after_attn)
    normed_ffn = rms_scale(whole_after, ffn_gain)
    gate_proj = times_rows(normed_ffn, gate_full)
    up_proj = times_rows(normed_ffn, up_full)
    activation = (jax.nn.silu(gate_proj) * up_proj).astype(jnp.bfloat16)
    summed = lax.psum_scatter(
        lax.dot_general(
            down_full, activation, (((0,), (1,)), ((), ())), preferred_element_type=jnp.float32
        ),
        "wide",
        scatter_dimension=0,
        tiled=True,
    )
    hidden_out = (after_attn.astype(jnp.float32) + summed.T).astype(jnp.bfloat16)
    offset = (slot_pos - length) % WINDOW
    fresh_slot = offset < span_len
    pick_row = jnp.minimum(offset, span_len - 1)
    new_k_cache = jnp.where(fresh_slot[:, None], jnp.take(new_keys, pick_row, axis=0), cache_keys)[
        None
    ]
    new_v_cache = jnp.where(fresh_slot[:, None], jnp.take(new_vals, pick_row, axis=0), cache_vals)[
        None
    ]
    return (hidden_out, new_k_cache, new_v_cache)


def solution(mesh):
    return jax.shard_map(
        per_device,
        mesh=mesh,
        in_specs=(
            P("narrow", "wide"),
            P(),
            P("narrow", "wide", None),
            P("narrow", "wide", None),
            P(),
            P(),
            P("wide", "narrow"),
            P("wide", "narrow"),
            P("wide", "narrow"),
            P("wide", "narrow"),
            P("wide", "narrow"),
        ),
        out_specs=(P("narrow", "wide"), P("narrow", "wide", None), P("narrow", "wide", None)),
        check_vma=False,
    )
```

profile of v0, /device:TPU:2, one launch (start us, length us, event | category | flops | bytes accessed | tf_op | source)
XLA Modules:
  0.0 569.9 jit_solution(13301387686112721194)
XLA Ops:
  7.2 0.7 all-gather.7.cloned.1.call-update
  8.0 1.3 dynamic_slice.37
  9.2 1.2 fusion.63
  10.5 1.2 fusion.64
  11.7 0.7 convert_element_type.93
  13.1 2.0 fusion.58
  15.0 0.6 iota_add_fusion.1
  15.7 14.4 %all_gather.25 = bf16[96,4096]{1,0:T(8,128)(2,1)S(1)} all-gather(bf16[96,1024]{1,0:T(8,128)(2,1)} %param.23), channel_id=1, replica_groups=mesh['wide'=64,'narrow'=4] {'narrow'}, dimensions={1}, use_global_device_ids=true | all-gather | bytes 983040 | tf_op jit(solution)/shard_map/all_gather | solution.py:141
  30.1 61.0 %all-gather.7.cloned.1.call-done = bf16[256,4096]{0,1:T(8,128)(2,1)} async-done(((bf16[256,64]{0,1:T(8,128)(2,1)}), bf16[256,4096]{0,1:T(8,128)(2,1)}) %all-gather.7.cloned.1.call-update) | async-done | bytes 2097168 | tf_op jit(solution)/shard_map/all_gather | solution.py:54
  91.0 2.3 fusion.16
  93.4 0.8 fusion.27
  94.2 0.4 collective-permute-start
  94.6 1.9 and_reduce_fusion
  97.9 0.7 broadcast_in_dim.114
  98.5 0.6 collective-permute-start.1
  99.2 4.4 collective-permute-done.1
  103.6 2.2 collective-permute-start.2
  106.1 5.3 collective-permute-done.2
  111.6 0.6 fusion.69
  113.1 0.6 pad_maximum_fusion.1
  113.9 11.8 %conditional.2 = ((f32[256,4]{1,0:T(8,128)S(1)}, f32[256,4]{1,0:T(8,128)}, f32[256,4,128]{2,0,1:T(8,128)S(1)})) conditional(s32[]{:T(128)} %convert_element_type.91, (f32[256,4]{1,0:T(8,128)S(1)}, f32[256,4]{1,0:T(8,128)}, f32[256,4,128]{2,0,1:T(8,128)S(1)}) %tuple.31, (pred[512]{0:T(512)(128)(4,1)S(1)}, s32[512]{0:T(512)S(1)}, s32[256]{0:T(256)S(1)}, ...), branch_computations={%region_5.6_spmd, %region_6.9_spmd} | conditional | flops 273942784 | bytes 13486680 | solution.py:125
  114.2 0.5 broadcast_in_dim.64
  114.6 0.5 broadcast_in_dim.65
  115.1 1.5 fusion
  116.6 0.8 reduce_max.28
  117.4 1.6 max.12
  119.0 1.0 sub.66
  120.0 1.8 fusion.1
  122.0 1.7 multiply_add_fusion
  123.7 1.4 dot_general.9
  125.1 0.6 convolution_add_fusion
  125.7 4.8 conditional.3
  125.8 0.7 compare_and_fusion.1
  126.9 0.9 copy.56
  128.6 0.9 multiply_add_fusion.1
  130.6 0.5 collective-permute-start.3
  131.2 1.3 collective-permute-done.3
  132.6 0.6 collective-permute-start.6
  133.2 1.5 collective-permute-start.10
  134.7 0.5 collective-permute-start.5
  135.2 11.6 %collective-permute-done.10 = f32[256,4]{0,1:T(4,128)S(1)} collective-permute-done((f32[256,4]{0,1:T(4,128)S(1)}, f32[256,4]{0,1:T(4,128)S(1)}, u32[]{:S(2)}, u32[]{:S(2)}) %collective-permute-start.10) | collective-permute-done | bytes 4128 | tf_op jit(solution)/shard_map/ppermute | solution.py:20
  147.1 3.5 collective-permute-start.11
  150.7 11.1 %collective-permute-done.11 = f32[256,4]{0,1:T(4,128)S(1)} collective-permute-done((f32[256,4]{0,1:T(4,128)S(1)}, f32[256,4]{0,1:T(4,128)S(1)}, u32[]{:S(2)}, u32[]{:S(2)}) %collective-permute-start.11) | collective-permute-done | bytes 4128 | tf_op jit(solution)/shard_map/ppermute | solution.py:20
  162.0 0.6 constant_dynamic-slice_fusion
  162.7 12.8 %all_gather.27 = bf16[64,4096]{1,0:T(8,128)(2,1)S(1)} all-gather(bf16[64,1024]{1,0:T(8,128)(2,1)S(1)} %copy-done.14), channel_id=1, replica_groups=mesh['wide'=64,'narrow'=4] {'narrow'}, dimensions={1}, use_global_device_ids=true | all-gather | bytes 655360 | tf_op jit(solution)/shard_map/all_gather | solution.py:142
  175.5 61.0 %all-gather.9.cloned.1.call-done = bf16[256,4096]{0,1:T(8,128)(2,1)} async-done(((bf16[256,64]{0,1:T(8,128)(2,1)}), bf16[256,4096]{0,1:T(8,128)(2,1)}) %all-gather.9.cloned.1.call-update) | async-done | bytes 2097168 | tf_op jit(solution)/shard_map/all_gather | solution.py:54
  236.4 2.7 fusion.30
  239.2 0.5 all-gather.13.cloned.1.call-update
  239.8 0.5 all-gather.15.cloned.1.call-update
  240.3 0.5 all-gather.17.cloned.1.call-update
  240.9 73.8 %all-gather.11.cloned.1.call-done = bf16[256,4096]{0,1:T(8,128)(2,1)} async-done(((bf16[256,64]{0,1:T(8,128)(2,1)}), bf16[256,4096]{0,1:T(8,128)(2,1)}) %all-gather.11.cloned.1.call-update) | async-done | bytes 2097168 | tf_op jit(solution)/shard_map/all_gather | solution.py:54
  314.8 2.3 fusion.19
  317.1 27.2 %all-gather.13.cloned.1.call-done = bf16[224,4096]{1,0:T(8,128)(2,1)} async-done(((bf16[224,1024]{1,0:T(8,128)(2,1)}), bf16[224,4096]{1,0:T(8,128)(2,1)}) %all-gather.13.cloned.1.call-update) | async-done | bytes 1835024 | tf_op jit(solution)/shard_map/all_gather | solution.py:143
  344.4 2.3 fusion.31
  346.7 30.5 %all-gather.15.cloned.1.call-done = bf16[224,4096]{1,0:T(8,128)(2,1)} async-done(((bf16[224,1024]{1,0:T(8,128)(2,1)}), bf16[224,4096]{1,0:T(8,128)(2,1)}) %all-gather.15.cloned.1.call-update) | async-done | bytes 1835024 | tf_op jit(solution)/shard_map/all_gather | solution.py:144
  377.3 32.9 %all-gather.17.cloned.1.call-done = bf16[224,4096]{1,0:T(8,128)(2,1)} async-done(((bf16[224,1024]{1,0:T(8,128)(2,1)}), bf16[224,4096]{1,0:T(8,128)(2,1)}) %all-gather.17.cloned.1.call-update) | async-done | bytes 1835024 | tf_op jit(solution)/shard_map/all_gather | solution.py:145
  410.2 6.4 %convolution_bitcast_fusion = f32[4096,256]{1,0:T(8,128)} fusion(bf16[224,4096]{1,0:T(8,128)(2,1)} %all-gather.17.cloned.1.call-done, bf16[224,4096]{1,0:T(8,128)(2,1)} %all-gather.15.cloned.1.call-done, bf16[256,4096]{0,1:T(8,128)(2,1)S(1)} %copy-done, f32[4096]{0:T(1024)S(1)} %convert_element_type.105, f32[256]{0:T(256)S(1)} %add_rsqrt_fusion, ...), kind=kOutput, calls=%fused_computation.32 | convolution fusion | flops 944062464 | bytes 10208256 | tf_op jit(solution)/shard_map/dot_general | solution.py:202
  416.6 0.7 compare_and_fusion.2
  417.3 0.6 compare_select_fusion
  418.2 1.3 gather_fusion
  419.6 1.3 gather_fusion.1
  420.9 0.9 fusion.40
  421.9 139.7 %reduce-scatter.2.cloned.1.call-done = f32[64,256]{1,0:T(8,128)} async-done(((f32[4096,256]{1,0:T(8,128)}), f32[64,256]{1,0:T(8,128)}) %reduce-scatter.2.cloned.1.call-update) | async-done | bytes 65552 | tf_op jit(solution)/shard_map/reduce_scatter | solution.py:201
  561.6 1.5 fusion.52
  (103 shorter events, 5.4 us)
Async XLA Ops:
  7.2 83.9 %all-gather.7.cloned.1.call-start = ((), (), s32[]{:S(2)}) async-start(), calls=%async_computation.1 | async-start | bytes 2129920 | tf_op jit(solution)/shard_map/all_gather | solution.py:54
  7.9 228.5 %all-gather.9.cloned.1.call-start = ((), (), s32[]{:S(2)}) async-start(), calls=%async_computation.2 | async-start | bytes 2129920 | tf_op jit(solution)/shard_map/all_gather | solution.py:54
  91.0 2.3 copy-start.1
  94.2 4.3 collective-permute-start
  98.5 5.0 collective-permute-start.1
  103.6 7.8 %collective-permute-start.2 = (bf16[256,384]{0,1:T(8,128)(2,1)S(1)}, bf16[256,384]{0,1:T(8,128)(2,1)S(1)}, u32[]{:S(2)}, u32[]{:S(2)}) collective-permute-start(bf16[256,384]{0,1:T(8,128)(2,1)S(1)} %maximum_select_fusion.1), channel_id=1, source_target_pairs={{0,16},{16,0},{4,20},{20,4},{8,24},{24,8},{12,28},{28,12},{32,48},... | collective-permute-start | bytes 589832 | tf_op jit(solution)/shard_map/ppermute | solution.py:20
  112.6 1.3 copy-start.9
  112.6 1.3 copy-start.11
  121.8 3.3 copy-start.7
  123.7 2.0 copy-start.2
  125.7 4.1 copy-start.4
  130.5 2.0 collective-permute-start.4
  130.6 1.9 collective-permute-start.3
  131.1 1.4 collective-permute-start.9
  132.5 30.2 %copy-start.14 = (bf16[64,1024]{1,0:T(8,128)(2,1)S(1)}, bf16[64,1024]{1,0:T(8,128)(2,1)}, u32[]{:S(2)}) copy-start(bf16[64,1024]{1,0:T(8,128)(2,1)} %param.24) | copy-start | bytes 393220
  132.6 103.8 %copy-start.13 = (bf16[256,64]{0,1:T(8,128)(2,1)S(1)}, bf16[256,64]{0,1:T(8,128)(2,1)}, u32[]{:S(2)}) copy-start(bf16[256,64]{0,1:T(8,128)(2,1)} %param.17) | copy-start | bytes 98308
  132.6 14.2 %collective-permute-start.6 = (f32[256,4,128]{0,2,1:T(8,128)S(1)}, f32[256,4,128]{0,2,1:T(8,128)S(1)}, u32[]{:S(2)}, u32[]{:S(2)}) collective-permute-start(f32[256,4,128]{0,2,1:T(8,128)S(1)} %multiply_add_fusion.3), channel_id=1, source_target_pairs={{0,8},{8,0},{4,12},{12,4},{16,24},{24,16},{20,28},{28,20},{32,40},... | collective-permute-start | bytes 1572872 | tf_op jit(solution)/shard_map/ppermute | solution.py:20
  133.2 13.6 %collective-permute-start.10 = (f32[256,4]{0,1:T(4,128)S(1)}, f32[256,4]{0,1:T(4,128)S(1)}, u32[]{:S(2)}, u32[]{:S(2)}) collective-permute-start(f32[256,4]{0,1:T(4,128)S(1)} %get-tuple-element.243), channel_id=1, source_target_pairs={{0,8},{8,0},{4,12},{12,4},{16,24},{24,16},{20,28},{28,20},{32,40},... | collective-permute-start | bytes 12296 | tf_op jit(solution)/shard_map/ppermute | solution.py:20
  134.7 12.1 %collective-permute-start.5 = (f32[256,4]{0,1:T(4,128)S(1)}, f32[256,4]{0,1:T(4,128)S(1)}, u32[]{:S(2)}, u32[]{:S(2)}) collective-permute-start(f32[256,4]{0,1:T(4,128)S(1)} %get-tuple-element.246), channel_id=1, source_target_pairs={{0,8},{8,0},{4,12},{12,4},{16,24},{24,16},{20,28},{28,20},{32,40},... | collective-permute-start | bytes 12296 | tf_op jit(solution)/shard_map/ppermute | solution.py:20
  147.0 14.9 %collective-permute-start.8 = (f32[256,4,128]{0,2,1:T(8,128)S(1)}, f32[256,4,128]{0,2,1:T(8,128)S(1)}, u32[]{:S(2)}, u32[]{:S(2)}) collective-permute-start(f32[256,4,128]{0,2,1:T(8,128)S(1)} %multiply_add_fusion.2), channel_id=1, source_target_pairs={{0,16},{16,0},{4,20},{20,4},{8,24},{24,8},{12,28},{28,12},{32,48},... | collective-permute-start | bytes 1572872 | tf_op jit(solution)/shard_map/ppermute | solution.py:20
  147.1 14.8 %collective-permute-start.11 = (f32[256,4]{0,1:T(4,128)S(1)}, f32[256,4]{0,1:T(4,128)S(1)}, u32[]{:S(2)}, u32[]{:S(2)}) collective-permute-start(f32[256,4]{0,1:T(4,128)S(1)} %get-tuple-element.239), channel_id=1, source_target_pairs={{0,16},{16,0},{4,20},{20,4},{8,24},{24,8},{12,28},{28,12},{32,48},... | collective-permute-start | bytes 12296 | tf_op jit(solution)/shard_map/ppermute | solution.py:20
  150.6 11.3 %collective-permute-start.7 = (f32[256,4]{0,1:T(4,128)S(1)}, f32[256,4]{0,1:T(4,128)S(1)}, u32[]{:S(2)}, u32[]{:S(2)}) collective-permute-start(f32[256,4]{0,1:T(4,128)S(1)} %get-tuple-element.242), channel_id=1, source_target_pairs={{0,16},{16,0},{4,20},{20,4},{8,24},{24,8},{12,28},{28,12},{32,48},... | collective-permute-start | bytes 12296 | tf_op jit(solution)/shard_map/ppermute | solution.py:20
  162.6 152.1 %all-gather.11.cloned.1.call-start = ((), (), s32[]{:S(2)}) async-start(), calls=%async_computation.3 | async-start | bytes 2129920 | tf_op jit(solution)/shard_map/all_gather | solution.py:54
  175.5 65.5 %copy-start.15 = (bf16[4096]{0:T(1024)(128)(2,1)S(1)}, bf16[4096]{0:T(1024)(128)(2,1)}, u32[]{:S(2)}) copy-start(bf16[4096]{0:T(1024)(128)(2,1)} %param.22) | copy-start | bytes 24580
  239.1 105.2 %all-gather.13.cloned.1.call-start = ((), (), s32[]{:S(2)}) async-start(), calls=%async_computation.4 | async-start | bytes 2293760 | tf_op jit(solution)/shard_map/all_gather | solution.py:143
  239.7 137.5 %all-gather.15.cloned.1.call-start = ((), (), s32[]{:S(2)}) async-start(), calls=%async_computation.5 | async-start | bytes 2293760 | tf_op jit(solution)/shard_map/all_gather | solution.py:144
  240.3 169.9 %all-gather.17.cloned.1.call-start = ((), (), s32[]{:S(2)}) async-start(), calls=%async_computation.6 | async-start | bytes 2293760 | tf_op jit(solution)/shard_map/all_gather | solution.py:145
  240.9 320.7 %reduce-scatter.2.cloned.1.call-start = ((), (), s32[]{:S(2)}) async-start(), calls=%async_computation.7 | async-start | bytes 4259840 | tf_op jit(solution)/shard_map/reduce_scatter | solution.py:201
  314.8 29.6 %copy-start = (bf16[256,4096]{0,1:T(8,128)(2,1)S(1)}, bf16[256,4096]{0,1:T(8,128)(2,1)}, u32[]{:S(2)}) copy-start(bf16[256,4096]{0,1:T(8,128)(2,1)} %all-gather.11.cloned.1.call-done) | copy-start | bytes 6291460
  416.5 1.4 copy-start.3
  416.5 1.6 copy-start.10
  416.5 1.6 copy-start.12
  416.6 4.4 copy-start.5
  416.6 4.4 copy-start.6
  416.6 145.0 %copy-start.8 = (bf16[256,64]{0,1:T(8,128)(2,1)S(1)}, bf16[256,64]{0,1:T(8,128)(2,1)}, u32[]{:S(2)}) copy-start(bf16[256,64]{0,1:T(8,128)(2,1)} %fusion.30) | copy-start | bytes 98308
Sparse Core Ops, SparseCore 0:
  10.8 80.2 all-gather.6
  162.8 73.6 all-gather.8
  239.8 74.9 all-gather.10
  316.4 27.8 all-gather.12
  346.0 31.1 all-gather.14
  378.9 31.1 all-gather.16
  416.7 144.8 reduce-scatter.1
where the time goes:
time: 570 us
  waiting for transfers between devices  462 us (81%)
  blocking collectives  27.1 us (5%)
  other arithmetic  25.7 us (5%)
  between operations  16.5 us (3%)
  matrix products  14.7 us (3%)
  local copies, waits for them, and re-layouts  12.8 us (2%)
  starting transfers between devices  10.4 us (2%)
    all_gather x3, waiting for transfers between devices, gather_cols(): return lax.all_gather(block, 'wide', axis=1, tiled=True)  196 us
    reduce_scatter x1, waiting for transfers between devices, per_device(): lax.psum_scatter(lax.dot_general(down_full, activation, (((0,), (1,)), ((...  140 us
    ppermute x12, waiting for transfers between devices, partner(): return lax.ppermute(block, axis, route)  33.9 us
    all_gather x1, waiting for transfers between devices, per_device(): lax.all_gather(wdown, 'narrow', axis=1, tiled=True)  32.9 us
    all_gather x1, waiting for transfers between devices, per_device(): lax.all_gather(wup, 'narrow', axis=1, tiled=True)  30.5 us
    all_gather x1, waiting for transfers between devices, per_device(): lax.all_gather(wgate, 'narrow', axis=1, tiled=True)  27.2 us
    all_gather x1, blocking collectives, per_device(): lax.all_gather(wqkv, 'narrow', axis=1, tiled=True)  14.4 us
    all_gather x1, blocking collectives, per_device(): lax.all_gather(wo, 'narrow', axis=1, tiled=True)  12.8 us
  transfers between devices with their start and end apart: 19, of which 12 were waited for; matrix products, arithmetic and copies ran while one was open for 3% of the time, Pallas kernels for 0%

commit v1 on v0

--- a/solution.py
+++ b/solution.py
@@ -137,12 +137,19 @@
 def per_device(
     hidden_in, cached_len, k_cache, v_cache, attn_gain, ffn_gain, wqkv, wo, wgate, wup, wdown
 ):
+
+    def zones_step_on(mine):
+        grid = []
+        for _ in range(jax.lax.axis_size("narrow")):
+            grid.append(mine)
+        return jnp.concatenate(jax.lax.all_to_all(jnp.stack(grid, 0), "narrow", 0, 0), 1)
+
     qkv_full, out_full, gate_full, up_full, down_full = (
         lax.all_gather(wqkv, "narrow", axis=1, tiled=True),
         lax.all_gather(wo, "narrow", axis=1, tiled=True),
         lax.all_gather(wgate, "narrow", axis=1, tiled=True),
         lax.all_gather(wup, "narrow", axis=1, tiled=True),
-        lax.all_gather(wdown, "narrow", axis=1, tiled=True),
+        zones_step_on(wdown),
     )
     wide_count = lax.axis_size("wide")
     part_count = wide_count // KVH

time: 570 us -> 539 us (0.946)
  waiting for transfers between devices: 462 us -> 422 us
    all_gather x1 -> x0, waiting for transfers between devices: 32.9 us -> none  [per_device(): lax.all_gather(wdown, 'narrow', axis=1, tiled=True)]
    all_gather x3, waiting for transfers between devices: 196 us -> 166 us  [gather_cols(): return lax.all_gather(block, 'wide', axis=1, tiled=True)]
    all_to_all x0 -> x1, waiting for transfers between devices: none -> 22.5 us  [zones_step_on(): jax.lax.all_to_all(jnp.stack(grid, 0), 'narrow', 0, 0)]
  transfers between devices with their start and end apart: 19 -> 19, of which waited for: 12 -> 12; matrix products, arithmetic and copies ran while one was open for 3% -> 4% of each run, Pallas kernels for 0% -> 0%
where the time goes in v1:
time: 539 us; the launch traced here: 538 us
  waiting for transfers between devices  422 us (78%)
  blocking collectives  27.3 us (5%)
  other arithmetic  25.2 us (5%)
  local copies, waits for them, and re-layouts  16.6 us (3%)
  between operations  16.5 us (3%)
  starting transfers between devices  15.4 us (3%)
  matrix products  14.7 us (3%)
    all_gather x3, waiting for transfers between devices, gather_cols(): return lax.all_gather(block, 'wide', axis=1, tiled=True)  166 us
    reduce_scatter x1, waiting for transfers between devices, per_device(): lax.psum_scatter(lax.dot_general(down_full, activation, (((0,), (1,)), ((...  140 us
    ppermute x12, waiting for transfers between devices, partner(): return lax.ppermute(block, axis, route)  33.8 us
    all_gather x1, waiting for transfers between devices, per_device(): lax.all_gather(wup, 'narrow', axis=1, tiled=True)  30.5 us
    all_gather x1, waiting for transfers between devices, per_device(): lax.all_gather(wgate, 'narrow', axis=1, tiled=True)  27.2 us
    all_to_all x1, waiting for transfers between devices, zones_step_on(): jax.lax.all_to_all(jnp.stack(grid, 0), 'narrow', 0, 0)  22.5 us
    all_gather x1, blocking collectives, per_device(): lax.all_gather(wqkv, 'narrow', axis=1, tiled=True)  14.4 us
    all_gather x1, blocking collectives, per_device(): lax.all_gather(wo, 'narrow', axis=1, tiled=True)  12.9 us
  transfers between devices with their start and end apart: 19, of which 12 were waited for; matrix products, arithmetic and copies ran while one was open for 4% of the time, Pallas kernels for 0%

profile of v1, /device:TPU:2, one launch (start us, length us, event | category | flops | bytes accessed | tf_op | source)
XLA Modules:
  0.0 538.0 jit_solution(15047786613520731180)
XLA Ops:
  7.2 0.7 all-gather.6.cloned.1.call-update
  7.9 1.2 dynamic_slice.37
  9.2 1.2 fusion.63
  10.4 1.2 fusion.64
  11.6 0.7 convert_element_type.93
  12.9 1.9 fusion.58
  14.8 0.6 iota_add_fusion.1
  15.4 14.4 %all_gather.22 = bf16[96,4096]{1,0:T(8,128)(2,1)S(1)} all-gather(bf16[96,1024]{1,0:T(8,128)(2,1)} %param.23), channel_id=1, replica_groups=mesh['wide'=64,'narrow'=4] {'narrow'}, dimensions={1}, use_global_device_ids=true | all-gather | bytes 983040 | tf_op jit(solution)/shard_map/all_gather | solution.py:148
  29.8 61.3 %all-gather.6.cloned.1.call-done = bf16[256,4096]{0,1:T(8,128)(2,1)} async-done(((bf16[256,64]{0,1:T(8,128)(2,1)}), bf16[256,4096]{0,1:T(8,128)(2,1)}) %all-gather.6.cloned.1.call-update) | async-done | bytes 2097168 | tf_op jit(solution)/shard_map/all_gather | solution.py:54
  91.0 2.3 fusion.16
  93.4 0.8 fusion.27
  94.6 1.8 and_reduce_fusion
  97.8 0.7 broadcast_in_dim.114
  98.5 0.6 collective-permute-start.1
  99.1 4.4 collective-permute-done.1
  103.6 2.2 collective-permute-start.2
  106.1 5.3 collective-permute-done.2
  111.6 0.6 fusion.69
  113.3 0.6 pad_maximum_fusion.1
  113.9 12.6 %conditional.2 = ((f32[256,4]{1,0:T(8,128)S(1)}, f32[256,4]{1,0:T(8,128)}, f32[256,4,128]{2,0,1:T(8,128)S(1)})) conditional(s32[]{:T(128)} %convert_element_type.91, (f32[256,4]{1,0:T(8,128)S(1)}, f32[256,4]{1,0:T(8,128)}, f32[256,4,128]{2,0,1:T(8,128)S(1)}) %tuple.31, (pred[512]{0:T(512)(128)(4,1)S(1)}, s32[512]{0:T(512)S(1)}, s32[256]{0:T(256)S(1)}, ...), branch_computations={%region_5.6_spmd, %region_6.9_spmd} | conditional | flops 273942784 | bytes 13470268 | solution.py:125
  115.1 1.5 fusion
  116.6 0.8 reduce_max.28
  117.4 1.6 max.12
  119.0 1.0 sub.66
  120.0 1.8 fusion.1
  121.9 1.7 multiply_add_fusion
  123.6 0.9 copy.108
  124.5 1.3 dot_general.9
  125.9 0.6 convolution_add_fusion
  126.5 4.8 conditional.3
  126.5 0.7 compare_and_fusion.1
  127.7 0.9 copy.80
  129.5 0.9 multiply_add_fusion.1
  131.3 0.5 collective-permute-start.9
  131.9 1.3 collective-permute-done.9
  133.4 0.8 collective-permute-start.6
  134.1 1.5 collective-permute-start.10
  135.7 0.5 collective-permute-start.5
  136.2 11.6 %collective-permute-done.10 = f32[256,4]{0,1:T(4,128)S(1)} collective-permute-done((f32[256,4]{0,1:T(4,128)S(1)}, f32[256,4]{0,1:T(4,128)S(1)}, u32[]{:S(2)}, u32[]{:S(2)}) %collective-permute-start.10) | collective-permute-done | bytes 4128 | tf_op jit(solution)/shard_map/ppermute | solution.py:20
  148.0 3.5 collective-permute-start.11
  151.6 11.1 %collective-permute-done.11 = f32[256,4]{0,1:T(4,128)S(1)} collective-permute-done((f32[256,4]{0,1:T(4,128)S(1)}, f32[256,4]{0,1:T(4,128)S(1)}, u32[]{:S(2)}, u32[]{:S(2)}) %collective-permute-start.11) | collective-permute-done | bytes 4128 | tf_op jit(solution)/shard_map/ppermute | solution.py:20
  162.9 0.6 constant_dynamic-slice_fusion
  163.6 12.9 %all_gather.24 = bf16[64,4096]{1,0:T(8,128)(2,1)S(1)} all-gather(bf16[64,1024]{1,0:T(8,128)(2,1)S(1)} %copy-done.14), channel_id=1, replica_groups=mesh['wide'=64,'narrow'=4] {'narrow'}, dimensions={1}, use_global_device_ids=true | all-gather | bytes 655360 | tf_op jit(solution)/shard_map/all_gather | solution.py:149
  176.5 60.8 %all-gather.8.cloned.1.call-done = bf16[256,4096]{0,1:T(8,128)(2,1)} async-done(((bf16[256,64]{0,1:T(8,128)(2,1)}), bf16[256,4096]{0,1:T(8,128)(2,1)}) %all-gather.8.cloned.1.call-update) | async-done | bytes 2097168 | tf_op jit(solution)/shard_map/all_gather | solution.py:54
  237.4 2.7 fusion.30
  240.1 0.5 all-gather.12.cloned.1.call-update
  240.7 0.5 all-gather.14.cloned.1.call-update
  241.2 1.5 stack.2
  242.7 4.9 all-to-all-start
  247.7 22.5 %all-to-all-done = bf16[4,224,1024]{2,1,0:T(8,128)(2,1)S(1)} async-done(((bf16[4,224,1024]{2,1,0:T(8,128)(2,1)}), bf16[4,224,1024]{2,1,0:T(8,128)(2,1)S(1)}, u32[]{:S(2)}, u32[]{:S(2)}) %all-to-all-start) | async-done | bytes 1835040 | tf_op jit(solution)/shard_map/all_to_all | solution.py:145
  270.1 1.5 copy.100
  271.6 44.1 %all-gather.10.cloned.1.call-done = bf16[256,4096]{0,1:T(8,128)(2,1)} async-done(((bf16[256,64]{0,1:T(8,128)(2,1)}), bf16[256,4096]{0,1:T(8,128)(2,1)}) %all-gather.10.cloned.1.call-update) | async-done | bytes 2097168 | tf_op jit(solution)/shard_map/all_gather | solution.py:54
  315.7 2.3 fusion.19
  318.0 27.2 %all-gather.12.cloned.1.call-done = bf16[224,4096]{1,0:T(8,128)(2,1)} async-done(((bf16[224,1024]{1,0:T(8,128)(2,1)}), bf16[224,4096]{1,0:T(8,128)(2,1)}) %all-gather.12.cloned.1.call-update) | async-done | bytes 1835024 | tf_op jit(solution)/shard_map/all_gather | solution.py:150
  345.3 2.3 fusion.31
  347.6 30.5 %all-gather.14.cloned.1.call-done = bf16[224,4096]{1,0:T(8,128)(2,1)} async-done(((bf16[224,1024]{1,0:T(8,128)(2,1)}), bf16[224,4096]{1,0:T(8,128)(2,1)}) %all-gather.14.cloned.1.call-update) | async-done | bytes 1835024 | tf_op jit(solution)/shard_map/all_gather | solution.py:151
  378.2 6.4 %convolution_bitcast_fusion = f32[4096,256]{1,0:T(8,128)} fusion(bf16[224,4096]{1,0:T(8,128)(2,1)} %bitcast.57, bf16[224,4096]{1,0:T(8,128)(2,1)} %all-gather.14.cloned.1.call-done, bf16[256,4096]{0,1:T(8,128)(2,1)S(1)} %copy-done, f32[4096]{0:T(1024)S(1)} %convert_element_type.105, f32[256]{0:T(256)S(1)} %add_rsqrt_fusion, f32[256,224]{0,1:T(8,128)S(1)} %fusion.31), kind=kOutput, calls=%fused_computation.32 | convolution fusion | flops 944062464 | bytes 10208256 | tf_op jit(solution)/shard_map/dot_general | solution.py:209
  384.6 0.7 compare_and_fusion.2
  385.2 0.6 compare_select_fusion
  386.1 1.3 gather_fusion.1
  387.5 1.3 gather_fusion
  388.8 0.9 fusion.40
  389.7 139.9 %reduce-scatter.2.cloned.1.call-done = f32[64,256]{1,0:T(8,128)} async-done(((f32[4096,256]{1,0:T(8,128)}), f32[64,256]{1,0:T(8,128)}) %reduce-scatter.2.cloned.1.call-update) | async-done | bytes 65552 | tf_op jit(solution)/shard_map/reduce_scatter | solution.py:208
  529.7 1.5 fusion.52
  (104 shorter events, 6.7 us)
Async XLA Ops:
  7.2 83.9 %all-gather.6.cloned.1.call-start = ((), (), s32[]{:S(2)}) async-start(), calls=%async_computation.2 | async-start | bytes 2129920 | tf_op jit(solution)/shard_map/all_gather | solution.py:54
  7.9 229.5 %all-gather.8.cloned.1.call-start = ((), (), s32[]{:S(2)}) async-start(), calls=%async_computation.3 | async-start | bytes 2129920 | tf_op jit(solution)/shard_map/all_gather | solution.py:54
  91.0 2.3 copy-start.1
  94.2 4.3 collective-permute-start
  98.5 5.0 collective-permute-start.1
  103.6 7.8 %collective-permute-start.2 = (bf16[256,384]{0,1:T(8,128)(2,1)S(1)}, bf16[256,384]{0,1:T(8,128)(2,1)S(1)}, u32[]{:S(2)}, u32[]{:S(2)}) collective-permute-start(bf16[256,384]{0,1:T(8,128)(2,1)S(1)} %maximum_select_fusion.1), channel_id=1, source_target_pairs={{0,16},{16,0},{4,20},{20,4},{8,24},{24,8},{12,28},{28,12},{32,48},... | collective-permute-start | bytes 589832 | tf_op jit(solution)/shard_map/ppermute | solution.py:20
  113.1 0.8 copy-start.9
  113.1 0.8 copy-start.11
  121.8 4.1 copy-start.6
  126.5 4.0 copy-start.3
  131.3 2.0 collective-permute-start.4
  131.3 1.9 collective-permute-start.9
  131.8 1.4 collective-permute-start.3
  133.3 30.3 %copy-start.14 = (bf16[64,1024]{1,0:T(8,128)(2,1)S(1)}, bf16[64,1024]{1,0:T(8,128)(2,1)}, u32[]{:S(2)}) copy-start(bf16[64,1024]{1,0:T(8,128)(2,1)} %param.24) | copy-start | bytes 393220
  133.3 104.0 %copy-start.13 = (bf16[256,64]{0,1:T(8,128)(2,1)S(1)}, bf16[256,64]{0,1:T(8,128)(2,1)}, u32[]{:S(2)}) copy-start(bf16[256,64]{0,1:T(8,128)(2,1)} %param.17) | copy-start | bytes 98308
  133.4 14.4 %collective-permute-start.6 = (f32[256,4,128]{0,2,1:T(8,128)S(1)}, f32[256,4,128]{0,2,1:T(8,128)S(1)}, u32[]{:S(2)}, u32[]{:S(2)}) collective-permute-start(f32[256,4,128]{0,2,1:T(8,128)S(1)} %multiply_add_fusion.3), channel_id=1, source_target_pairs={{0,8},{8,0},{4,12},{12,4},{16,24},{24,16},{20,28},{28,20},{32,40},... | collective-permute-start | bytes 1572872 | tf_op jit(solution)/shard_map/ppermute | solution.py:20
  134.1 13.6 %collective-permute-start.10 = (f32[256,4]{0,1:T(4,128)S(1)}, f32[256,4]{0,1:T(4,128)S(1)}, u32[]{:S(2)}, u32[]{:S(2)}) collective-permute-start(f32[256,4]{0,1:T(4,128)S(1)} %get-tuple-element.252), channel_id=1, source_target_pairs={{0,8},{8,0},{4,12},{12,4},{16,24},{24,16},{20,28},{28,20},{32,40},... | collective-permute-start | bytes 12296 | tf_op jit(solution)/shard_map/ppermute | solution.py:20
  135.7 12.1 %collective-permute-start.5 = (f32[256,4]{0,1:T(4,128)S(1)}, f32[256,4]{0,1:T(4,128)S(1)}, u32[]{:S(2)}, u32[]{:S(2)}) collective-permute-start(f32[256,4]{0,1:T(4,128)S(1)} %get-tuple-element.255), channel_id=1, source_target_pairs={{0,8},{8,0},{4,12},{12,4},{16,24},{24,16},{20,28},{28,20},{32,40},... | collective-permute-start | bytes 12296 | tf_op jit(solution)/shard_map/ppermute | solution.py:20
  147.9 14.9 %collective-permute-start.8 = (f32[256,4,128]{0,2,1:T(8,128)S(1)}, f32[256,4,128]{0,2,1:T(8,128)S(1)}, u32[]{:S(2)}, u32[]{:S(2)}) collective-permute-start(f32[256,4,128]{0,2,1:T(8,128)S(1)} %multiply_add_fusion.2), channel_id=1, source_target_pairs={{0,16},{16,0},{4,20},{20,4},{8,24},{24,8},{12,28},{28,12},{32,48},... | collective-permute-start | bytes 1572872 | tf_op jit(solution)/shard_map/ppermute | solution.py:20
  148.0 14.7 %collective-permute-start.11 = (f32[256,4]{0,1:T(4,128)S(1)}, f32[256,4]{0,1:T(4,128)S(1)}, u32[]{:S(2)}, u32[]{:S(2)}) collective-permute-start(f32[256,4]{0,1:T(4,128)S(1)} %get-tuple-element.248), channel_id=1, source_target_pairs={{0,16},{16,0},{4,20},{20,4},{8,24},{24,8},{12,28},{28,12},{32,48},... | collective-permute-start | bytes 12296 | tf_op jit(solution)/shard_map/ppermute | solution.py:20
  151.5 11.3 %collective-permute-start.7 = (f32[256,4]{0,1:T(4,128)S(1)}, f32[256,4]{0,1:T(4,128)S(1)}, u32[]{:S(2)}, u32[]{:S(2)}) collective-permute-start(f32[256,4]{0,1:T(4,128)S(1)} %get-tuple-element.251), channel_id=1, source_target_pairs={{0,16},{16,0},{4,20},{20,4},{8,24},{24,8},{12,28},{28,12},{32,48},... | collective-permute-start | bytes 12296 | tf_op jit(solution)/shard_map/ppermute | solution.py:20
  163.5 77.7 %copy-start.7 = (bf16[224,1024]{1,0:T(8,128)(2,1)S(1)}, bf16[224,1024]{1,0:T(8,128)(2,1)}, u32[]{:S(2)}) copy-start(bf16[224,1024]{1,0:T(8,128)(2,1)} %param.27) | copy-start | bytes 1376260
  163.5 152.1 %all-gather.10.cloned.1.call-start = ((), (), s32[]{:S(2)}) async-start(), calls=%async_computation.4 | async-start | bytes 2129920 | tf_op jit(solution)/shard_map/all_gather | solution.py:54
  240.0 105.2 %all-gather.12.cloned.1.call-start = ((), (), s32[]{:S(2)}) async-start(), calls=%async_computation.5 | async-start | bytes 2293760 | tf_op jit(solution)/shard_map/all_gather | solution.py:150
  240.6 137.5 %all-gather.14.cloned.1.call-start = ((), (), s32[]{:S(2)}) async-start(), calls=%async_computation.6 | async-start | bytes 2293760 | tf_op jit(solution)/shard_map/all_gather | solution.py:151
  242.7 5.0 copy-start.15
  242.7 27.4 %all-to-all-start = ((bf16[4,224,1024]{2,1,0:T(8,128)(2,1)}), bf16[4,224,1024]{2,1,0:T(8,128)(2,1)S(1)}, u32[]{:S(2)}, u32[]{:S(2)}) async-start(bf16[4,224,1024]{2,1,0:T(8,128)(2,1)} %stack.2), calls=%async_computation | async-start | bytes 3670016 | tf_op jit(solution)/shard_map/all_to_all | solution.py:145
  247.7 282.0 %reduce-scatter.2.cloned.1.call-start = ((), (), s32[]{:S(2)}) async-start(), calls=%async_computation.7 | async-start | bytes 4259840 | tf_op jit(solution)/shard_map/reduce_scatter | solution.py:208
  315.7 29.6 %copy-start = (bf16[256,4096]{0,1:T(8,128)(2,1)S(1)}, bf16[256,4096]{0,1:T(8,128)(2,1)}, u32[]{:S(2)}) copy-start(bf16[256,4096]{0,1:T(8,128)(2,1)} %all-gather.10.cloned.1.call-done) | copy-start | bytes 6291460
  384.5 1.3 copy-start.2
  384.5 1.4 copy-start.10
  384.5 1.4 copy-start.12
  384.6 4.3 copy-start.4
  384.6 4.3 copy-start.5
  384.6 145.1 %copy-start.8 = (bf16[256,64]{0,1:T(8,128)(2,1)S(1)}, bf16[256,64]{0,1:T(8,128)(2,1)}, u32[]{:S(2)}) copy-start(bf16[256,64]{0,1:T(8,128)(2,1)} %fusion.30) | copy-start | bytes 98308
Sparse Core Ops, SparseCore 0:
  10.8 80.2 all-gather.5
  163.7 73.6 all-gather.7
  240.7 74.9 all-gather.9
  317.4 27.8 all-gather.11
  346.9 31.1 all-gather.13
  384.7 144.9 reduce-scatter.1
